TPU v7x, 512 devices: a whole 4x4x16 slice. The times are simulated.
512 devices in a mesh: ctx: 16 (over y, x), head: 32 (over z, core).
Axes of the slice: x: 4, y: 4, z: 16, core: 2. Of those that a mesh axis runs over, the one named last changes fastest.
Arguments:
- doc_lengths: int32 [4], replicated, may hold values from 1 to 6144, 8192 in all
- lin_q: bfloat16 [8192, 8192], P('ctx', 'head'), may hold values from -6 to 6
- lin_k: bfloat16 [8192, 8192], P('ctx', 'head'), may hold values from -6 to 6
- lin_v: bfloat16 [8192, 8192], P('ctx', 'head'), may hold values from -40 to 40
- log_decay: float32 [64, 8192], P('head', 'ctx'), may hold values from -1 to 0
- lin_gain: float32 [8192], P('head'), may hold values from 0.5 to 1.5
- soft_q: bfloat16 [8192, 8192], P('ctx', 'head'), may hold values from -48 to 48
- soft_k: bfloat16 [8192, 1024], P('ctx', 'head'), may hold values from -6 to 6
- soft_v: bfloat16 [8192, 1024], P('ctx', 'head'), may hold values from -6 to 6
Outputs:
- lin_out: bfloat16 [8192, 8192], P('ctx', 'head')
- soft_out: bfloat16 [8192, 8192], P('ctx', 'head')
Inputs may be any that keep to these rules, and one draw needn't show every extreme that they name: `doc_lengths`: the 4 lengths sum to 8192 and the largest is exactly 6144.
All inputs are finite; a program needn't handle non-finite values.
Results may differ from a plain program's by a relative error of at most 0.015.
Values may be sent and summed in bfloat16 or wider, within the bound.
A program may use at most 64 MiB of HBM per device.

v0:
```python
import jax
import jax.numpy as jnp
from jax import lax
from jax.sharding import PartitionSpec as P

KVH = 8
DH = 128
BLK = 256


def prefix(value, axis, join, neutral):
    place = lax.axis_index(axis)
    gathered = jax.tree.map(
        lambda a, kind: lax.all_gather(a.astype(kind), axis), value, (jnp.bfloat16, jnp.bfloat16)
    )
    state = jax.tree.map(lambda a, e: jnp.zeros_like(a) + jnp.asarray(e, a.dtype), value, neutral)

    def one(turn, state):
        return join(
            state,
            jax.tree.map(
                lambda a, own: lax.dynamic_index_in_dim(a, turn, 0, False).astype(own.dtype),
                gathered,
                value,
            ),
        )

    return lax.fori_loop(0, place, one, state)


def swapped(value, axis, stride):
    return lax.ppermute(value, axis, [(i, i ^ 1 << stride) for i in range(lax.axis_size(axis))])


def doc_index(doc_lengths, positions):
    bounds = jnp.cumsum(doc_lengths)
    counted = jnp.sum((bounds[None, :] <= positions[:, None]).astype(jnp.int32), axis=1)
    return jnp.where(positions < 0, -1, counted)


def lightning_parts(queries, keys_block, values_block, decay_block, segs_block, seg_before):
    running = jnp.cumsum(decay_block, axis=1)
    block_len = segs_block.shape[0]
    rows_iota = lax.broadcasted_iota(jnp.int32, (block_len, block_len), 0)
    cols_iota = lax.broadcasted_iota(jnp.int32, (block_len, block_len), 1)
    allowed = (rows_iota >= cols_iota) & (segs_block[:, None] == segs_block[None, :])
    spread = jnp.where(allowed[None], running[:, :, None] - running[:, None, :], 0.0)
    decays = jnp.where(allowed[None], jnp.exp(spread), 0.0)
    scores = (
        jnp.einsum("ihd,jhd->hij", queries, keys_block, preferred_element_type=jnp.float32) * decays
    )
    scores = scores.astype(jnp.bfloat16)
    inside = jnp.einsum("hij,jhd->ihd", scores, values_block, preferred_element_type=jnp.float32)
    carried = (segs_block == seg_before).astype(jnp.float32)
    entering = jnp.exp(running) * carried[None, :]
    closing = running[:, -1:]
    tail_mask = (segs_block == segs_block[-1]).astype(jnp.float32)
    weights = jnp.exp(closing - running) * tail_mask[None, :]
    weighted = (keys_block * weights.T[:, :, None]).astype(jnp.bfloat16)
    update = jnp.einsum("jhd,jhe->hde", weighted, values_block, preferred_element_type=jnp.float32)
    kept_flag = (segs_block[-1] == seg_before).astype(jnp.float32)
    decay_factor = kept_flag * jnp.exp(closing[:, 0])
    return (inside, entering, update, decay_factor)


def local(doc_lengths, lin_q, lin_k, lin_v, log_decay, lin_gain, soft_q, soft_k, soft_v):
    tok_count = lin_q.shape[0]
    heads_here = lin_gain.shape[0] // DH
    ctx_place = lax.axis_index("ctx")
    positions = ctx_place * tok_count + jnp.arange(tok_count, dtype=jnp.int32)
    doc_ids = doc_index(doc_lengths, positions)
    seg_previous = doc_index(doc_lengths, positions[:1] - 1)[0]
    query_rows = lin_q.reshape(tok_count, heads_here, DH)
    key_rows = lin_k.reshape(tok_count, heads_here, DH)
    value_rows = lin_v.reshape(tok_count, heads_here, DH)
    blocks = tok_count // BLK
    pieces_list = []
    local_state = jnp.zeros((heads_here, DH, DH), jnp.float32)
    through = jnp.ones((heads_here,), jnp.float32)
    for number in range(blocks):
        first_row = number * BLK
        last_row = first_row + BLK
        seg_before = seg_previous if number == 0 else doc_ids[first_row - 1]
        parts_now = lightning_parts(
            query_rows[first_row:last_row],
            key_rows[first_row:last_row],
            value_rows[first_row:last_row],
            log_decay[:, first_row:last_row],
            doc_ids[first_row:last_row],
            seg_before,
        )
        pieces_list.append(parts_now)
        local_state = parts_now[3][:, None, None] * local_state + parts_now[2]
        through = through * parts_now[3]
    empty_state = jnp.zeros((heads_here, DH, DH), jnp.float32)

    def combine(earlier, later):
        return (earlier[0] * later[0], later[0][:, None, None] * earlier[1] + later[1])

    incoming = prefix(
        (through, local_state), "ctx", combine, (jnp.ones((heads_here,), jnp.float32), empty_state)
    )
    carry_state = incoming[1]
    outputs = []
    for number in range(blocks):
        first_row = number * BLK
        inside, entering, update, decay_factor = pieces_list[number]
        across = jnp.einsum(
            "ihd,hde->ihe",
            query_rows[first_row : first_row + BLK],
            carry_state.astype(jnp.bfloat16),
            preferred_element_type=jnp.float32,
        )
        outputs.append(inside + across * entering.T[:, :, None])
        carry_state = decay_factor[:, None, None] * carry_state + update
    raw_out = jnp.concatenate(outputs, axis=0)
    norm_scale = lax.rsqrt(jnp.mean(raw_out * raw_out, axis=2, keepdims=True) + 1e-06)
    lin_out = (
        (raw_out * norm_scale * lin_gain.reshape(1, heads_here, DH))
        .reshape(tok_count, heads_here * DH)
        .astype(jnp.bfloat16)
    )
    head_place = lax.axis_index("head")
    group_width = lax.axis_size("head") // KVH
    bit_count = group_width.bit_length() - 1
    own_keys, own_values = (soft_k, soft_v)
    for bit in range(bit_count):
        far_keys, far_values = swapped((own_keys, own_values), "head", bit)
        upper = head_place // (1 << bit) % 2 == 1
        own_keys = jnp.where(
            upper,
            jnp.concatenate([far_keys, own_keys], axis=1),
            jnp.concatenate([own_keys, far_keys], axis=1),
        )
        own_values = jnp.where(
            upper,
            jnp.concatenate([far_values, own_values], axis=1),
            jnp.concatenate([own_values, far_values], axis=1),
        )
    soft_rows = soft_q.reshape(tok_count, heads_here, DH)

    def attend(softmax_state, key_piece, value_piece, key_start):
        row_top, row_total, accum_rows = softmax_state
        key_pos = key_start + jnp.arange(key_piece.shape[0], dtype=jnp.int32)
        key_doc = doc_index(doc_lengths, key_pos)
        scores = jnp.einsum(
            "ihd,jd->hij", soft_rows, key_piece, preferred_element_type=jnp.float32
        ) * DH ** (-0.5)
        allowed = (key_pos[None, :] <= positions[:, None]) & (key_doc[None, :] == doc_ids[:, None])
        masked = jnp.where(allowed[None], scores, -1e30)
        new_top = jnp.maximum(row_top, jnp.max(masked, axis=2))
        exp_terms = jnp.where(allowed[None], jnp.exp(scores - new_top[:, :, None]), 0.0)
        rescale = jnp.exp(row_top - new_top)
        new_total = rescale * row_total + jnp.sum(exp_terms, axis=2)
        new_accum = rescale[:, :, None] * accum_rows + jnp.einsum(
            "hij,jd->hid",
            exp_terms.astype(jnp.bfloat16),
            value_piece,
            preferred_element_type=jnp.float32,
        )
        return (new_top, new_total, new_accum)

    def visit(softmax_state, key_piece, value_piece, key_start):
        return attend(softmax_state, key_piece, value_piece, key_start)

    start_state = (
        jnp.full((heads_here, tok_count), -1e30, jnp.float32),
        jnp.zeros((heads_here, tok_count), jnp.float32),
        jnp.zeros((heads_here, tok_count, DH), jnp.float32),
    )
    key_piece = lax.all_gather(own_keys, "ctx", axis=0, tiled=True)
    value_piece = lax.all_gather(own_values, "ctx", axis=0, tiled=True)
    row_count = key_piece.shape[0]

    def inner_visit(state_in, scan_items):
        offset, key_part, value_part = scan_items
        return (visit(state_in, key_part, value_part, offset), None)

    offsets = jnp.arange(row_count // 512, dtype=jnp.int32) * 512
    result, _ = lax.scan(
        inner_visit,
        start_state,
        (
            offsets,
            key_piece.reshape(row_count // 512, 512, DH),
            value_piece.reshape(row_count // 512, 512, DH),
        ),
    )
    final_top, final_total, final_accum = result
    soft_out = (
        (final_accum / final_total[:, :, None])
        .transpose(1, 0, 2)
        .reshape(tok_count, heads_here * DH)
        .astype(jnp.bfloat16)
    )
    return (lin_out, soft_out)


def solution(mesh):
    placed = (
        P(),
        P("ctx", "head"),
        P("ctx", "head"),
        P("ctx", "head"),
        P("head", "ctx"),
        P("head"),
        P("ctx", "head"),
        P("ctx", "head"),
        P("ctx", "head"),
    )
    return jax.shard_map(
        local,
        mesh=mesh,
        in_specs=placed,
        out_specs=(P("ctx", "head"), P("ctx", "head")),
        check_vma=False,
    )
```

profile of v0, /device:TPU:25, one launch (start us, length us, event | category | flops | bytes accessed | tf_op | source)
XLA Modules:
  0.0 322.0 jit_solution(9549522584730469660)
XLA Ops:
  21.5 2.6 collective-permute-start
  24.9 3.5 %collective-permute-start.1 = (bf16[512,64]{0,1:T(8,128)(2,1)S(1)}, bf16[512,64]{0,1:T(8,128)(2,1)S(1)}, u32[]{:S(2)}, u32[]{:S(2)}) collective-permute-start(bf16[512,64]{0,1:T(8,128)(2,1)S(1)} %maximum_select_fusion.2), channel_id=1, source_target_pairs={{0,2},{1,3},{2,0},{3,1},{4,6},{5,7},{6,4},{7,5},{8,10},{9,11},{10,... | collective-permute-start | bytes 196616 | tf_op jit(solution)/shard_map/ppermute | solution.py:32
  28.5 2.0 collective-permute-done.1
  31.3 2.9 collective-permute-start.2
  35.0 3.5 %collective-permute-start.3 = (bf16[512,64]{0,1:T(8,128)(2,1)S(1)}, bf16[512,64]{0,1:T(8,128)(2,1)S(1)}, u32[]{:S(2)}, u32[]{:S(2)}) collective-permute-start(bf16[512,64]{0,1:T(8,128)(2,1)S(1)} %maximum_select_fusion.3), channel_id=1, source_target_pairs={{0,2},{1,3},{2,0},{3,1},{4,6},{5,7},{6,4},{7,5},{8,10},{9,11},{10,... | collective-permute-start | bytes 196616 | tf_op jit(solution)/shard_map/ppermute | solution.py:32
  38.5 1.6 collective-permute-done.3
  43.1 27.4 %all-reduce = bf16[32]{0:T(256)(128)(2,1)S(1)} all-reduce(bf16[32]{0:T(256)(128)(2,1)S(1)} %dynamic-update-slice), channel_id=2, replica_groups=mesh['ctx'=16,'head'=32] {'ctx'}, use_global_device_ids=true, to_apply=%add | all-reduce | flops 32 | bytes 128
  71.5 10.4 %all-gather.10.cloned.1.call-done = bf16[32,128,128]{2,1,0:T(8,128)(2,1)} async-done(((bf16[2,128,128]{2,1,0:T(8,128)(2,1)}), bf16[32,128,128]{2,1,0:T(8,128)(2,1)}) %all-gather.10.cloned.1.call-update) | async-done | bytes 1048592 | tf_op jit(solution)/shard_map/all_gather | solution.py:14
  82.0 11.7 %while.29 = (s32[]{:T(128)}, f32[2,128,128]{2,1,0:T(8,128)S(1)}, s32[]{:T(128)}, bf16[16,2]{1,0:T(8,128)(2,1)S(1)}, bf16[16,2,128,128]{3,2,1,0:T(8,128)(2,1)}, /*index=5*/s32[]{:T(128)}, s32[]{:T(128)}, s32[]{:T(128)}) while((s32[]{:T(128)}, f32[2,128,128]{2,1,0:T(8,128)S(1)}, s32[]{:T(128)}, bf16[16,2]{1,0:T(8,128)(2,1)S(1)}, ...), condition=%wide.region_8.9_spmd, body=%wide.region_7.8_spmd.sunk | while | flops 98311 | bytes 327827 | solution.py:28
  97.1 51.4 %all-gather.6.cloned.1.call-done = bf16[8192,128]{0,1:T(8,128)(2,1)} async-done(((bf16[512,128]{0,1:T(8,128)(2,1)}), bf16[8192,128]{0,1:T(8,128)(2,1)}) %all-gather.6.cloned.1.call-update) | async-done | bytes 2097168 | tf_op jit(solution)/shard_map/all_gather | solution.py:171
  148.5 4.1 %copy.122 = bf16[8192,128]{1,0:T(8,128)(2,1)} copy(bf16[8192,128]{0,1:T(8,128)(2,1)} %all-gather.6.cloned.1.call-done) | data formatting | bytes 4194304 | tf_op jit(solution)/shard_map/all_gather | solution.py:171
  152.6 61.4 %all-gather.8.cloned.1.call-done = bf16[8192,128]{0,1:T(8,128)(2,1)} async-done(((bf16[512,128]{0,1:T(8,128)(2,1)}), bf16[8192,128]{0,1:T(8,128)(2,1)}) %all-gather.8.cloned.1.call-update) | async-done | bytes 2097168 | tf_op jit(solution)/shard_map/all_gather | solution.py:172
  214.0 4.1 %copy.124 = bf16[8192,128]{1,0:T(8,128)(2,1)} copy(bf16[8192,128]{0,1:T(8,128)(2,1)} %all-gather.8.cloned.1.call-done) | data formatting | bytes 4194304 | tf_op jit(solution)/shard_map/all_gather | solution.py:172
  218.1 96.5 %while.30 = (s32[]{:T(128)}, f32[2,512]{1,0:T(2,128)S(1)}, f32[2,512]{1,0:T(2,128)S(1)}, f32[2,512,128]{2,1,0:T(8,128)S(1)}, s32[16]{0:T(128)S(1)}, /*index=5*/s...) while((s32[]{:T(128)}, f32[2,512]{1,0:T(2,128)S(1)}, ...), condition=%wide.region_15.16_spmd.clone, body=%wide.region_11.15_spmd.clone.sunk | while | flops 275395584 | bytes 9000113 | solution.py:180
  220.3 1.5 fusion.92
  222.3 1.7 convolution_add_fusion.3
  226.4 1.5 fusion.92
  228.4 1.7 convolution_add_fusion.3
  234.4 1.7 convolution_add_fusion.3
  240.4 1.7 convolution_add_fusion.3
  246.5 1.7 convolution_add_fusion.3
  252.5 1.7 convolution_add_fusion.3
  258.5 1.7 convolution_add_fusion.3
  264.6 1.7 convolution_add_fusion.3
  270.6 1.7 convolution_add_fusion.3
  276.6 1.7 convolution_add_fusion.3
  282.6 1.7 convolution_add_fusion.3
  288.7 1.7 convolution_add_fusion.3
  294.7 1.7 convolution_add_fusion.3
  300.7 1.7 convolution_add_fusion.3
  306.8 1.7 convolution_add_fusion.3
  312.8 1.7 convolution_add_fusion.3
  (271 shorter events, 96.7 us)
Async XLA Ops:
  7.2 14.3 %copy-start.2 = (bf16[512,32]{0,1:T(8,128)(2,1)S(1)}, bf16[512,32]{0,1:T(8,128)(2,1)}, u32[]{:S(2)}) copy-start(bf16[512,32]{0,1:T(8,128)(2,1)} %param.20) | copy-start | bytes 98308
  7.2 24.1 %copy-start.3 = (bf16[512,32]{0,1:T(8,128)(2,1)S(1)}, bf16[512,32]{0,1:T(8,128)(2,1)}, u32[]{:S(2)}) copy-start(bf16[512,32]{0,1:T(8,128)(2,1)} %param.21) | copy-start | bytes 98308
  7.2 74.8 %all-gather.10.cloned.1.call-start = ((), (), s32[]{:S(2)}) async-start(), calls=%async_computation.2 | async-start | bytes 1114112 | tf_op jit(solution)/shard_map/all_gather | solution.py:14
  17.8 52.7 %copy-start = (bf16[512,256]{1,0:T(8,128)(2,1)S(1)}, bf16[512,256]{1,0:T(8,128)(2,1)}, u32[]{:S(2)}) copy-start(bf16[512,256]{1,0:T(8,128)(2,1)} %param.19) | copy-start | bytes 786436
  19.9 50.9 %copy-start.5 = (s32[4]{0:T(128)S(1)}, s32[4]{0:T(128)}, u32[]{:S(2)}) copy-start(s32[4]{0:T(128)} %param.13) | copy-start | bytes 52
  19.9 51.2 %copy-start.1 = (bf16[512,256]{1,0:T(8,128)(2,1)S(1)}, bf16[512,256]{1,0:T(8,128)(2,1)}, u32[]{:S(2)}) copy-start(bf16[512,256]{1,0:T(8,128)(2,1)} %param.14) | copy-start | bytes 786436
  21.4 127.1 %all-gather.6.cloned.1.call-start = ((), (), s32[]{:S(2)}) async-start(), calls=%async_computation | async-start | bytes 2228224 | tf_op jit(solution)/shard_map/all_gather | solution.py:171
  21.5 3.4 %collective-permute-start = (bf16[512,32]{0,1:T(8,128)(2,1)S(1)}, bf16[512,32]{0,1:T(8,128)(2,1)S(1)}, u32[]{:S(2)}, u32[]{:S(2)}) collective-permute-start(bf16[512,32]{0,1:T(8,128)(2,1)S(1)} %copy-done.2), channel_id=1, source_target_pairs={{0,1},{1,0},{2,3},{3,2},{4,5},{5,4},{6,7},{7,6},{8,9},{9,8},{10,11... | collective-permute-start | bytes 98312 | tf_op jit(solution)/shard_map/ppermute | solution.py:32
  24.9 5.6 %collective-permute-start.1 = (bf16[512,64]{0,1:T(8,128)(2,1)S(1)}, bf16[512,64]{0,1:T(8,128)(2,1)S(1)}, u32[]{:S(2)}, u32[]{:S(2)}) collective-permute-start(bf16[512,64]{0,1:T(8,128)(2,1)S(1)} %maximum_select_fusion.2), channel_id=1, source_target_pairs={{0,2},{1,3},{2,0},{3,1},{4,6},{5,7},{6,4},{7,5},{8,10},{9,11},{10,... | collective-permute-start | bytes 196616 | tf_op jit(solution)/shard_map/ppermute | solution.py:32
  31.2 182.8 %all-gather.8.cloned.1.call-start = ((), (), s32[]{:S(2)}) async-start(), calls=%async_computation.1 | async-start | bytes 2228224 | tf_op jit(solution)/shard_map/all_gather | solution.py:172
  31.3 3.7 %collective-permute-start.2 = (bf16[512,32]{0,1:T(8,128)(2,1)S(1)}, bf16[512,32]{0,1:T(8,128)(2,1)S(1)}, u32[]{:S(2)}, u32[]{:S(2)}) collective-permute-start(bf16[512,32]{0,1:T(8,128)(2,1)S(1)} %copy-done.3), channel_id=1, source_target_pairs={{0,1},{1,0},{2,3},{3,2},{4,5},{5,4},{6,7},{7,6},{8,9},{9,8},{10,11... | collective-permute-start | bytes 98312 | tf_op jit(solution)/shard_map/ppermute | solution.py:32
  35.0 5.1 %collective-permute-start.3 = (bf16[512,64]{0,1:T(8,128)(2,1)S(1)}, bf16[512,64]{0,1:T(8,128)(2,1)S(1)}, u32[]{:S(2)}, u32[]{:S(2)}) collective-permute-start(bf16[512,64]{0,1:T(8,128)(2,1)S(1)} %maximum_select_fusion.3), channel_id=1, source_target_pairs={{0,2},{1,3},{2,0},{3,1},{4,6},{5,7},{6,4},{7,5},{8,10},{9,11},{10,... | collective-permute-start | bytes 196616 | tf_op jit(solution)/shard_map/ppermute | solution.py:32
  94.7 1.6 copy-start.4
Sparse Core Ops, SparseCore 0:
  21.5 60.3 all-gather.9
  85.5 62.9 all-gather.5
  151.5 62.4 all-gather.7
where the time goes:
time: 326 us; the launch traced here: 322 us
  waiting for transfers between devices  129 us (40%)
  other arithmetic  54.4 us (17%)
  matrix products  53.5 us (16%)
  blocking collectives  27.4 us (8%)
  local copies, waits for them, and re-layouts  25.8 us (8%)
  between operations  18.1 us (6%)
  starting transfers between devices  12.6 us (4%)
    all_gather x1, waiting for transfers between devices, local(): value_piece = lax.all_gather(own_values, 'ctx', axis=0, tiled=True)  61.4 us
    all_gather x1, waiting for transfers between devices, local(): key_piece = lax.all_gather(own_keys, 'ctx', axis=0, tiled=True)  51.4 us
    dot_general x16, matrix products, attend(): jnp.einsum('hij,jd->hid', exp_terms.astype(jnp.bfloat16), value_piece, pr...  27.7 us
    unnamed x1, blocking collectives  27.4 us
    dot_general x16, matrix products, attend(): jnp.einsum('ihd,jd->hij', soft_rows, key_piece, preferred_element_type=jn...  23.3 us
    ppermute x4, starting transfers between devices, swapped(): lax.ppermute(value, axis, [(i, i ^ 1 << stride) for i in range(lax.axis_s...  12.5 us
    add x12, other arithmetic, combine(): later[0][:, None, None] * earlier[1] + later[1]  11.2 us
    all_gather x1, waiting for transfers between devices, prefix(): lax.all_gather(a.astype(kind), axis)  10.4 us
  transfers between devices with their start and end apart: 7, of which 7 were waited for; matrix products, arithmetic and copies ran while one was open for 7% of the time, Pallas kernels for 0%

commit v1 on v0

v1 whole, which is shorter than its diff:
```python
import math

import jax
import jax.numpy as jnp
from jax import lax
from jax.experimental import pallas as pl
from jax.experimental.pallas import tpu as pltpu
from jax.sharding import PartitionSpec as P

DH = 128
BLK = 256
TOK = 512
REACH = 12
HALF = 256
BIG = 1048576.0
SCALE = math.log2(math.e) / math.sqrt(DH)
MESH = pl.DeviceIdType.MESH
F32 = jnp.float32
BF16 = jnp.bfloat16
AB = (((1,), (0,)), ((), ()))
ABT = (((1,), (1,)), ((), ()))
ATB = (((0,), (0,)), ((), ()))


def mm(a, b, dims=AB):
    return lax.dot_general(a, b, dims, preferred_element_type=F32)


def kernel(
    doc, lq_in, lk_in, lv_in, ld_in, gain_in, sq_in, sk_in, sv_in,
    lin_out, soft_out,
    lq, lk, lv, ld, gain, sq,
    kv, qx, top, acc, raw, cum, row_st, col_st, first_up, carry,
    in_sem, x_send, x_recv, s_send, s_recv, z_send, z_recv, t_send, t_recv,
    r_send, r_recv, c_send, c_recv,
):
    me = lax.axis_index("ctx")
    hd = lax.axis_index("head")
    col, line = lax.rem(me, 4), me // 4
    sib = hd + 1 - 2 * lax.rem(hd, 2)
    zp = hd + 2 - 4 * lax.rem(hd // 2, 2)
    quarter = lax.rem(hd, 4)
    zquarter = lax.rem(zp, 4)
    n_lo = jnp.minimum(me, REACH)
    n_hi = jnp.minimum(15 - me, REACH)

    loads = [
        pltpu.make_async_copy(a, b, in_sem.at[i])
        for i, (a, b) in enumerate(
            [(sk_in, kv.at[0, quarter, :32]), (sv_in, kv.at[0, quarter, 32:]), (sq_in, sq), (lq_in, lq), (lk_in, lk), (lv_in, lv), (ld_in, ld), (gain_in, gain)]
        )
    ]
    for load in loads:
        load.start()

    barrier = pltpu.get_barrier_semaphore()

    def greet(ctx, head):
        pl.semaphore_signal(barrier, inc=1, device_id=(ctx, head), device_id_type=MESH)

    greet(me, sib)
    greet(me, zp)
    lax.fori_loop(1, n_lo + 1, lambda d, c: (greet(me - d, hd), c)[1], 0)
    lax.fori_loop(1, n_hi + 1, lambda d, c: (greet(me + d, hd), c)[1], 0)

    loads[0].wait()
    loads[1].wait()
    pl.semaphore_wait(barrier, 2 + n_lo + n_hi)

    def copy(src, dst, send, recv, ctx, head):
        return pltpu.make_async_remote_copy(
            src_ref=src, dst_ref=dst, send_sem=send, recv_sem=recv, device_id=(ctx, head), device_id_type=MESH
        )

    def x_copy(d):
        return copy(kv.at[0, quarter], kv.at[d, quarter], x_send.at[d], x_recv.at[d], me + d, hd)

    def s_copy(d):
        return copy(kv.at[d, quarter], kv.at[d, quarter], s_send.at[d], s_recv.at[d], me, sib)

    def z_copy(d):
        return copy(kv.at[d, quarter], kv.at[d, quarter], z_send.at[d], z_recv.at[d], me, zp)

    def t_copy(d):
        return copy(kv.at[d, zquarter], kv.at[d, zquarter], t_send.at[d], t_recv.at[d], me, sib)

    def r_copy(k):
        return copy(row_st.at[0], row_st.at[k], r_send.at[k], r_recv.at[k], line * 4 + lax.rem(col + k, 4), hd)

    def c_copy(k):
        return copy(col_st.at[0], col_st.at[k], c_send.at[k], c_recv.at[k], me + 4 * k, hd)

    def pass_own(d):
        @pl.when(d <= n_lo)
        def _():
            x_copy(d).wait_recv()
            s_copy(d).start()
            z_copy(d).start()

    def pass_far(d):
        @pl.when(d <= n_lo)
        def _():
            z_copy(d).wait_recv()
            t_copy(d).start()

    s_copy(0).start()
    z_copy(0).start()
    lax.fori_loop(1, n_hi + 1, lambda d, c: (x_copy(d).start(), c)[1], 0)

    bounds = [doc[0], doc[0] + doc[1], doc[0] + doc[1] + doc[2]]

    def doc_start(p):
        start = jnp.zeros_like(p)
        for b in bounds:
            start = jnp.maximum(start, jnp.where(b <= p, b, 0))
        return start

    def doc_id(p):
        count = jnp.zeros_like(p)
        for b in bounds:
            count = count + jnp.where(b <= p, 1, 0)
        return count

    base = me * TOK

    loads[2].wait()
    rows = base + lax.broadcasted_iota(jnp.int32, (TOK, DH), 0)
    lanes = lax.broadcasted_iota(jnp.int32, (TOK, DH), 1)
    marks = jnp.where(doc_id(rows) == lanes, 1.0, 0.0).astype(BF16)
    for h in range(2):
        qx[h * TOK : (h + 1) * TOK, :DH] = sq[:, h * DH : (h + 1) * DH]
        qx[h * TOK : (h + 1) * TOK, DH:] = marks

    for load in loads[3:]:
        load.wait()
    tri = jnp.where(
        lax.broadcasted_iota(jnp.int32, (BLK, BLK), 0) <= lax.broadcasted_iota(jnp.int32, (BLK, BLK), 1), 1.0, 0.0
    ).astype(F32)
    steps = jnp.concatenate([ld[:, :BLK], ld[:, BLK:], jnp.zeros((4, BLK), F32)], axis=0)
    running = lax.dot_general(steps, tri, AB, precision=lax.Precision.HIGHEST, preferred_element_type=F32)
    cum[...] = running.T
    row_of = lax.broadcasted_iota(jnp.int32, (BLK, BLK), 0)
    col_of = lax.broadcasted_iota(jnp.int32, (BLK, BLK), 1)
    col_pos = lax.broadcasted_iota(jnp.int32, (BLK, 1), 0)

    def parts(b, h):
        r = slice(b * BLK, (b + 1) * BLK)
        c = slice(h * DH, (h + 1) * DH)
        return r, c, running[2 * b + h : 2 * b + h + 1, :], cum[:, 2 * b + h : 2 * b + h + 1]

    def through(b, h):
        end = running[2 * b + h : 2 * b + h + 1, BLK - 1 :]
        return jnp.exp(end)

    def kept(first, last):
        return jnp.where(doc_start(last) <= first - 1, 1.0, 0.0).astype(F32)

    for h in range(2):
        ups = []
        for b in range(2):
            r, c, across_row, down_col = parts(b, h)
            first = base + b * BLK
            start = doc_start(first + col_pos) - first
            allowed = (col_of <= row_of) & (col_of >= start)
            decays = jnp.exp(down_col - across_row)
            a = jnp.where(allowed, mm(lq[r, c], lk[r, c], ABT) * decays, 0.0).astype(BF16)
            raw[r, c] = mm(a, lv[r, c])
            tail = jnp.where(
                first + col_pos >= doc_start(first + BLK - 1), jnp.exp(across_row[:, BLK - 1 :] - down_col), 0.0
            )
            w = (lk[r, c].astype(F32) * tail).astype(BF16)
            ups.append(mm(w, lv[r, c], ATB))
        first_up[h] = ups[0]
        whole = kept(base + BLK, base + TOK - 1) * through(1, h) * ups[0] + ups[1]
        row_st[0, h * DH : (h + 1) * DH] = whole.astype(BF16)
    pad_row = lax.broadcasted_iota(jnp.int32, (16, DH), 0)

    def factor_rows(f0, f1):
        hi0, hi1 = f0.astype(BF16).astype(F32), f1.astype(BF16).astype(F32)
        out = jnp.where(pad_row == 0, hi0, 0.0)
        out = jnp.where(pad_row == 1, f0 - hi0, out)
        out = jnp.where(pad_row == 2, hi1, out)
        return jnp.where(pad_row == 3, f1 - hi1, out).astype(BF16)

    row_st[0, 2 * DH :] = factor_rows(through(0, 0) * through(1, 0), through(0, 1) * through(1, 1))
    for k in range(1, 4):
        r_copy(k).start()

    def factor_of(block, h):
        tail = block[2 * DH :].astype(F32)
        return tail[2 * h : 2 * h + 1] + tail[2 * h + 1 : 2 * h + 2]

    def keys_of(d):
        quarters = [kv[d, i, :32] for i in range(4)]
        ids = doc_id((me - d) * TOK + lax.broadcasted_iota(jnp.int32, (16, TOK), 1))
        which = lax.broadcasted_iota(jnp.int32, (16, TOK), 0)
        block = jnp.where((which < 4) & (which != ids), -BIG, 0.0).astype(BF16)
        return jnp.concatenate(quarters + [block, jnp.zeros((DH - 16, TOK), BF16)], axis=0)

    def values_of(d):
        quarters = [kv[d, i, 32:] for i in range(4)]
        return jnp.concatenate(quarters + [jnp.ones((DH, TOK), BF16)], axis=0)

    def arrived(d):
        s_copy(d).wait_recv()
        t_copy(d).wait_recv()

    def diagonal():
        keys, values = keys_of(0), values_of(0)
        for t in range(4):
            r = slice(t * HALF, (t + 1) * HALF)
            s = mm(qx[r], keys)
            pos = (t % 2) * HALF + lax.broadcasted_iota(jnp.int32, (HALF, TOK), 0)
            s = jnp.where(lax.broadcasted_iota(jnp.int32, (HALF, TOK), 1) <= pos, s, -BIG)
            m = jnp.max(s, axis=1, keepdims=True)
            p = jnp.exp2((s - m) * SCALE).astype(BF16)
            acc[r] = mm(p, values, ABT)
            top[r] = jnp.broadcast_to(m, (HALF, DH))

    def visit(d):
        keys, values = keys_of(d), values_of(d)
        for t in range(4):
            r = slice(t * HALF, (t + 1) * HALF)
            s = mm(qx[r], keys)
            old = top[r, :1]
            m = jnp.maximum(old, jnp.max(s, axis=1, keepdims=True))
            p = jnp.exp2((s - m) * SCALE).astype(BF16)
            acc[r] = jnp.exp2((old - m) * SCALE) * acc[r] + mm(p, values, ABT)
            top[r] = jnp.broadcast_to(m, (HALF, DH))

    pass_far(0)
    pass_own(1)
    arrived(0)
    diagonal()
    pass_far(1)
    pass_own(2)

    for k in range(1, 4):
        r_copy(k).wait_recv()
    line_first = line * 4 * TOK
    enter_row = []
    enter_factor = []
    for h in range(2):
        total = jnp.zeros((DH, DH), F32)
        before = jnp.zeros((DH, DH), F32)
        factor = jnp.ones((1, DH), F32)
        factor_before = jnp.ones((1, DH), F32)
        plain = jnp.ones((1, DH), F32)
        for x in range(4):
            block = row_st[lax.rem(col - x + 4, 4)]
            own = col == x
            before = jnp.where(own, total, before)
            factor_before = jnp.where(own, factor, factor_before)
            f = factor_of(block, h)
            fk = f * kept(line_first + x * TOK, line_first + (x + 1) * TOK - 1)
            total = fk * total + block[h * DH : (h + 1) * DH].astype(F32)
            factor = factor * fk
            plain = plain * f
        carry[h] = before
        enter_factor.append(factor_before)
        enter_row.append(plain)
        col_st[0, h * DH : (h + 1) * DH] = total.astype(BF16)
    col_st[0, 2 * DH :] = factor_rows(enter_row[0], enter_row[1])
    n_down = 3 - line
    lax.fori_loop(1, n_down + 1, lambda k, c: (c_copy(k).start(), c)[1], 0)

    def loop_body(d, c):
        pass_far(d + 1)
        pass_own(d + 2)
        arrived(d)
        visit(d)
        return c

    early = jnp.minimum(n_lo, 2)
    lax.fori_loop(1, early + 1, loop_body, 0)

    def column(i, state):
        k = line - i
        c_copy(k).wait_recv()
        block = col_st[k]
        first = i * 4 * TOK
        keep = kept(first, first + 4 * TOK - 1)
        return tuple(
            keep * factor_of(block, h) * state[h] + block[h * DH : (h + 1) * DH].astype(F32) for h in range(2)
        )

    entered = lax.fori_loop(0, line, column, (jnp.zeros((DH, DH), F32), jnp.zeros((DH, DH), F32)))
    for h in range(2):
        state = enter_factor[h] * entered[h] + carry[h]
        for b in range(2):
            r, c, _, down_col = parts(b, h)
            first = base + b * BLK
            mine = jnp.where(doc_start(first + col_pos) <= first - 1, jnp.exp(down_col), 0.0)
            full = raw[r, c] + mine * mm(lq[r, c], state.astype(BF16))
            scale = lax.rsqrt(jnp.mean(full * full, axis=1, keepdims=True) + 1e-6)
            lin_out[r, c] = (full * scale * gain[:, c]).astype(BF16)
            if b == 0:
                state = kept(base, base + BLK - 1) * through(0, h) * state + first_up[h]

    lax.fori_loop(early + 1, n_lo + 1, loop_body, 0)

    for t in range(4):
        r = slice(t * HALF, (t + 1) * HALF)
        out = acc[r, :DH] / acc[r, DH:]
        h, b = t // 2, t % 2
        soft_out[b * HALF : (b + 1) * HALF, h * DH : (h + 1) * DH] = out.astype(BF16)

    def sent(d, c):
        s_copy(d).wait_send()
        z_copy(d).wait_send()
        t_copy(d).wait_send()
        return c

    lax.fori_loop(0, n_lo + 1, sent, 0)
    lax.fori_loop(1, n_hi + 1, lambda d, c: (x_copy(d).wait_send(), c)[1], 0)
    for k in range(1, 4):
        r_copy(k).wait_send()
    lax.fori_loop(1, n_down + 1, lambda k, c: (c_copy(k).wait_send(), c)[1], 0)


def local(doc_lengths, lin_q, lin_k, lin_v, log_decay, lin_gain, soft_q, soft_k, soft_v):
    vmem = pltpu.VMEM
    dma = pltpu.SemaphoreType.DMA
    wide = (TOK, 2 * DH)
    slots = REACH + 1
    return pl.pallas_call(
        kernel,
        out_shape=(jax.ShapeDtypeStruct(wide, BF16), jax.ShapeDtypeStruct(wide, BF16)),
        in_specs=[pl.BlockSpec(memory_space=pltpu.SMEM)] + [pl.BlockSpec(memory_space=pl.ANY)] * 8,
        out_specs=(pl.BlockSpec(memory_space=vmem), pl.BlockSpec(memory_space=vmem)),
        scratch_shapes=[
            vmem(wide, BF16), vmem(wide, BF16), vmem(wide, BF16), vmem((2, TOK), F32), vmem((1, 2 * DH), F32),
            vmem(wide, BF16),
            vmem((slots, 4, 64, TOK), BF16), vmem((2 * TOK, 2 * DH), BF16), vmem((2 * TOK, DH), F32),
            vmem((2 * TOK, 2 * DH), F32), vmem(wide, F32), vmem((BLK, 8), F32),
            vmem((4, 2 * DH + 16, DH), BF16), vmem((4, 2 * DH + 16, DH), BF16), vmem((2, DH, DH), F32),
            vmem((2, DH, DH), F32),
            dma((8,)), dma((slots,)), dma((slots,)), dma((slots,)), dma((slots,)), dma((slots,)), dma((slots,)),
            dma((slots,)), dma((slots,)), dma((4,)), dma((4,)), dma((4,)), dma((4,)),
        ],
        compiler_params=pltpu.CompilerParams(
            collective_id=0, has_side_effects=True, vmem_limit_bytes=40 * 1024 * 1024
        ),
    )(doc_lengths, lin_q, lin_k, lin_v, log_decay, lin_gain.reshape(1, 2 * DH), soft_q, soft_k.T, soft_v.T)


def solution(mesh):
    both = P("ctx", "head")
    return jax.shard_map(
        local,
        mesh=mesh,
        in_specs=(P(), both, both, both, P("head", "ctx"), P("head"), both, both, both),
        out_specs=(both, both),
        check_vma=False,
    )
```

time: 326 us -> 65.1 us (0.20); the launches traced: 322 us -> 64.5 us
  waiting for transfers between devices: 129 us -> 0 us
  Pallas kernels: 0 us -> 56.5 us
  other arithmetic: 54.4 us -> 0 us
  matrix products: 53.5 us -> 0 us
  blocking collectives: 27.4 us -> 0 us
  local copies, waits for them, and re-layouts: 25.8 us -> 7.39 us
  between operations: 18.1 us -> 0.67 us
  starting transfers between devices: 12.6 us -> 0 us
    all_gather x3 -> x0, waiting for transfers between devices: 123 us -> none  [the longest x1 61.4 us: local(): value_piece = lax.all_gather(own_values, 'ctx', axis=0, tiled=True)]
    pallas_call x0 -> x1, Pallas kernels: none -> 56.5 us  [local(): pl.pallas_call(kernel, out_shape=(jax.ShapeDtypeStruct(wide, BF16), jax.S...]
    dot_general x38 -> x0, matrix products: 53.5 us -> none  [the longest x16 27.7 us: attend(): jnp.einsum('hij,jd->hid', exp_terms.astype(jnp.bfloat16), value_piece, pr...]
    unnamed x1 -> x0, blocking collectives: 27.4 us -> none
    add x45 -> x0, other arithmetic: 21.8 us -> none  [the longest x12 11.2 us: combine(): later[0][:, None, None] * earlier[1] + later[1]]
    ppermute x4 -> x0, starting transfers between devices: 12.5 us -> none  [swapped(): lax.ppermute(value, axis, [(i, i ^ 1 << stride) for i in range(lax.axis_s...]
    select_n x21 -> x0, other arithmetic: 11.8 us -> none  [the longest x17 10.4 us: doc_index(): return jnp.where(positions < 0, -1, counted)]
    reduce_sum x35 -> x0, other arithmetic: 10.1 us -> none  [the longest x16 7.97 us: attend(): new_total = rescale * row_total + jnp.sum(exp_terms, axis=2)]
  transfers between devices with their start and end apart: 7 -> 0, of which waited for: 7 -> 0; matrix products, arithmetic and copies ran while one was open for 7% -> 0% of each run, Pallas kernels for 0% -> 0%
where the time goes in v1:
time: 65.1 us; the launch traced here: 64.5 us
  Pallas kernels  56.5 us (87%)
  local copies, waits for them, and re-layouts  7.39 us (11%)
  between operations  0.67 us (1%)
    pallas_call x1, Pallas kernels, local(): pl.pallas_call(kernel, out_shape=(jax.ShapeDtypeStruct(wide, BF16), jax.S...  56.5 us
    unnamed x20, local copies, waits for them, and re-layouts  7.39 us

profile of v1, /device:TPU:25, one launch (start us, length us, event | category | flops | bytes accessed | tf_op | source)
XLA Modules:
  0.0 64.5 jit_solution(7119334555577284324)
XLA Ops:
  0.6 0.0 copy-start.6
  0.6 0.0 copy-start.7
  0.7 0.0 copy-start.8
  0.7 0.7 %copy-done.6 = f32[2,512]{1,0:T(2,128)S(1)} copy-done((f32[2,512]{1,0:T(2,128)S(1)}, f32[2,512]{1,0:T(2,128)}, u32[]{:S(2)}) %copy-start.6) | copy-done | bytes 4120
  1.3 0.0 copy-done.7
  1.3 0.0 copy-done.8
  1.3 0.0 copy-start
  1.3 0.9 %copy-done = bf16[512,256]{1,0:T(8,128)(2,1)S(1)} copy-done((bf16[512,256]{1,0:T(8,128)(2,1)S(1)}, bf16[512,256]{1,0:T(8,128)(2,1)}, u32[]{:S(2)}) %copy-start) | copy-done | bytes 262168
  2.3 0.0 copy-start.1
  2.3 0.9 %copy-done.1 = bf16[512,256]{1,0:T(8,128)(2,1)S(1)} copy-done((bf16[512,256]{1,0:T(8,128)(2,1)S(1)}, bf16[512,256]{1,0:T(8,128)(2,1)}, u32[]{:S(2)}) %copy-start.1) | copy-done | bytes 262168
  3.2 0.0 copy-start.2
  3.2 0.9 %copy-done.2 = bf16[512,256]{1,0:T(8,128)(2,1)S(1)} copy-done((bf16[512,256]{1,0:T(8,128)(2,1)S(1)}, bf16[512,256]{1,0:T(8,128)(2,1)}, u32[]{:S(2)}) %copy-start.2) | copy-done | bytes 262168
  4.2 0.0 copy-start.3
  4.2 0.9 %copy-done.3 = bf16[512,256]{1,0:T(8,128)(2,1)S(1)} copy-done((bf16[512,256]{1,0:T(8,128)(2,1)S(1)}, bf16[512,256]{1,0:T(8,128)(2,1)}, u32[]{:S(2)}) %copy-start.3) | copy-done | bytes 262168
  5.1 0.0 copy-start.4
  5.1 0.8 %copy-done.4 = bf16[512,32]{0,1:T(8,128)(2,1)S(1)} copy-done((bf16[512,32]{0,1:T(8,128)(2,1)S(1)}, bf16[512,32]{0,1:T(8,128)(2,1)}, u32[]{:S(2)}) %copy-start.4) | copy-done | bytes 32792
  5.9 0.0 copy-start.5
  5.9 0.8 %copy-done.5 = bf16[512,32]{0,1:T(8,128)(2,1)S(1)} copy-done((bf16[512,32]{0,1:T(8,128)(2,1)S(1)}, bf16[512,32]{0,1:T(8,128)(2,1)}, u32[]{:S(2)}) %copy-start.5) | copy-done | bytes 32792
  6.7 56.5 %shard_map.104 = (bf16[512,256]{1,0:T(8,128)(2,1)S(1)}, bf16[512,256]{1,0:T(8,128)(2,1)S(1)}) custom-call(s32[4]{0:T(128)S(1)} %copy-done.8, bf16[512,256]{1,0:T(8,128)(2,1)S(1)} %copy-done, bf16[512,256]{1,0:T(8,128)(2,1)S(1)} %copy-done.1, bf16[512,256]{1,0:T(8,128)(2,1)S(1)} %copy-done.2, f32[2,512]{1,0:T(2,128)S(1)} %copy-done.6, f32[1,256]{1,0:T(1,128)S(1)} %bitcast.5, ...), custom_call_target="tpu_custom_call" | custom-call | tf_op jit(solution)/shard_map/pallas_call | solution.py:326
  63.1 0.7 %copy.13 = bf16[512,256]{1,0:T(8,128)(2,1)} copy(bf16[512,256]{1,0:T(8,128)(2,1)S(1)} %get-tuple-element.4) | data formatting | bytes 524288
  63.8 0.7 %copy.14 = bf16[512,256]{1,0:T(8,128)(2,1)} copy(bf16[512,256]{1,0:T(8,128)(2,1)S(1)} %get-tuple-element.5) | data formatting | bytes 524288
Async XLA Ops:
  0.6 0.7 %copy-start.6 = (f32[2,512]{1,0:T(2,128)S(1)}, f32[2,512]{1,0:T(2,128)}, u32[]{:S(2)}) copy-start(f32[2,512]{1,0:T(2,128)} %ld_in.1) | copy-start | bytes 12292
  0.6 0.7 %copy-start.7 = (f32[256]{0:T(256)S(1)}, f32[256]{0:T(256)}, u32[]{:S(2)}) copy-start(f32[256]{0:T(256)} %param.14) | copy-start | bytes 3076
  0.7 0.7 %copy-start.8 = (s32[4]{0:T(128)S(1)}, s32[4]{0:T(128)}, u32[]{:S(2)}) copy-start(s32[4]{0:T(128)} %doc.1) | copy-start | bytes 52
  1.3 1.0 %copy-start = (bf16[512,256]{1,0:T(8,128)(2,1)S(1)}, bf16[512,256]{1,0:T(8,128)(2,1)}, u32[]{:S(2)}) copy-start(bf16[512,256]{1,0:T(8,128)(2,1)} %lq_in.1) | copy-start | bytes 786436
  2.3 0.9 %copy-start.1 = (bf16[512,256]{1,0:T(8,128)(2,1)S(1)}, bf16[512,256]{1,0:T(8,128)(2,1)}, u32[]{:S(2)}) copy-start(bf16[512,256]{1,0:T(8,128)(2,1)} %lk_in.1) | copy-start | bytes 786436
  3.2 0.9 %copy-start.2 = (bf16[512,256]{1,0:T(8,128)(2,1)S(1)}, bf16[512,256]{1,0:T(8,128)(2,1)}, u32[]{:S(2)}) copy-start(bf16[512,256]{1,0:T(8,128)(2,1)} %lv_in.1) | copy-start | bytes 786436
  4.2 0.9 %copy-start.3 = (bf16[512,256]{1,0:T(8,128)(2,1)S(1)}, bf16[512,256]{1,0:T(8,128)(2,1)}, u32[]{:S(2)}) copy-start(bf16[512,256]{1,0:T(8,128)(2,1)} %sq_in.1) | copy-start | bytes 786436
  5.1 0.8 %copy-start.4 = (bf16[512,32]{0,1:T(8,128)(2,1)S(1)}, bf16[512,32]{0,1:T(8,128)(2,1)}, u32[]{:S(2)}) copy-start(bf16[512,32]{0,1:T(8,128)(2,1)} %param.16) | copy-start | bytes 98308
  5.9 0.8 %copy-start.5 = (bf16[512,32]{0,1:T(8,128)(2,1)S(1)}, bf16[512,32]{0,1:T(8,128)(2,1)}, u32[]{:S(2)}) copy-start(bf16[512,32]{0,1:T(8,128)(2,1)} %param.17) | copy-start | bytes 98308

commit v2 on v1

--- a/solution.py
+++ b/solution.py
@@ -10,6 +10,8 @@
 DH = 128
 BLK = 256
 TOK = 512
+NEAR = 9
+LOOK = 4
 REACH = 12
 HALF = 256
 BIG = 1048576.0
@@ -31,7 +33,7 @@
     lin_out, soft_out,
     lq, lk, lv, ld, gain, sq,
     kv, qx, top, acc, raw, cum, row_st, col_st, first_up, carry,
-    in_sem, x_send, x_recv, s_send, s_recv, z_send, z_recv, t_send, t_recv,
+    in_sem, x_send, x_recv, y_send, s_send, s_recv, z_send, z_recv, t_send, t_recv,
     r_send, r_recv, c_send, c_recv,
 ):
     me = lax.axis_index("ctx")
@@ -75,6 +77,9 @@
     def x_copy(d):
         return copy(kv.at[0, quarter], kv.at[d, quarter], x_send.at[d], x_recv.at[d], me + d, hd)
 
+    def y_copy(d):
+        return copy(kv.at[0, zquarter], kv.at[d, zquarter], y_send.at[d], z_recv.at[d], me + d, hd)
+
     def s_copy(d):
         return copy(kv.at[d, quarter], kv.at[d, quarter], s_send.at[d], s_recv.at[d], me, sib)
 
@@ -95,7 +100,7 @@
         def _():
             x_copy(d).wait_recv()
             s_copy(d).start()
-            z_copy(d).start()
+            pl.when(d <= NEAR)(lambda: z_copy(d).start())
 
     def pass_far(d):
         @pl.when(d <= n_lo)
@@ -173,6 +178,10 @@
         first_up[h] = ups[0]
         whole = kept(base + BLK, base + TOK - 1) * through(1, h) * ups[0] + ups[1]
         row_st[0, h * DH : (h + 1) * DH] = whole.astype(BF16)
+        if h == 0:
+            pass_far(0)
+            lax.fori_loop(NEAR + 1, n_hi + 1, lambda d, c: (y_copy(d).start(), c)[1], 0)
+            pass_own(1)
     pad_row = lax.broadcasted_iota(jnp.int32, (16, DH), 0)
 
     def factor_rows(f0, f1):
@@ -228,12 +237,12 @@
             acc[r] = jnp.exp2((old - m) * SCALE) * acc[r] + mm(p, values, ABT)
             top[r] = jnp.broadcast_to(m, (HALF, DH))
 
-    pass_far(0)
-    pass_own(1)
+    pass_own(2)
     arrived(0)
     diagonal()
+    for d in range(3, LOOK + 1):
+        pass_own(d)
     pass_far(1)
-    pass_own(2)
 
     for k in range(1, 4):
         r_copy(k).wait_recv()
@@ -265,8 +274,8 @@
     lax.fori_loop(1, n_down + 1, lambda k, c: (c_copy(k).start(), c)[1], 0)
 
     def loop_body(d, c):
+        pass_own(d + LOOK)
         pass_far(d + 1)
-        pass_own(d + 2)
         arrived(d)
         visit(d)
         return c
@@ -307,12 +316,13 @@
 
     def sent(d, c):
         s_copy(d).wait_send()
-        z_copy(d).wait_send()
+        pl.when(d <= NEAR)(lambda: z_copy(d).wait_send())
         t_copy(d).wait_send()
         return c
 
     lax.fori_loop(0, n_lo + 1, sent, 0)
     lax.fori_loop(1, n_hi + 1, lambda d, c: (x_copy(d).wait_send(), c)[1], 0)
+    lax.fori_loop(NEAR + 1, n_hi + 1, lambda d, c: (y_copy(d).wait_send(), c)[1], 0)
     for k in range(1, 4):
         r_copy(k).wait_send()
     lax.fori_loop(1, n_down + 1, lambda k, c: (c_copy(k).wait_send(), c)[1], 0)
@@ -336,10 +346,10 @@
             vmem((4, 2 * DH + 16, DH), BF16), vmem((4, 2 * DH + 16, DH), BF16), vmem((2, DH, DH), F32),
             vmem((2, DH, DH), F32),
             dma((8,)), dma((slots,)), dma((slots,)), dma((slots,)), dma((slots,)), dma((slots,)), dma((slots,)),
-            dma((slots,)), dma((slots,)), dma((4,)), dma((4,)), dma((4,)), dma((4,)),
+            dma((slots,)), dma((slots,)), dma((slots,)), dma((4,)), dma((4,)), dma((4,)), dma((4,)),
         ],
         compiler_params=pltpu.CompilerParams(
-            collective_id=0, has_side_effects=True, vmem_limit_bytes=40 * 1024 * 1024
+            collective_id=0, has_side_effects=True, vmem_limit_bytes=60 * 1024 * 1024
         ),
     )(doc_lengths, lin_q, lin_k, lin_v, log_decay, lin_gain.reshape(1, 2 * DH), soft_q, soft_k.T, soft_v.T)
 

time: 65.1 us -> 48.7 us (0.75)
  Pallas kernels: 56.5 us -> 45.2 us
  local copies, waits for them, and re-layouts: 7.39 us -> 2.42 us
    pallas_call x1, Pallas kernels: 56.5 us -> 45.2 us  [local(): pl.pallas_call(kernel, out_shape=(jax.ShapeDtypeStruct(wide, BF16), jax.S...]
    unnamed x20 -> x4, local copies, waits for them, and re-layouts: 7.39 us -> 2.42 us
where the time goes in v2:
time: 48.7 us; the launch traced here: 48.2 us
  Pallas kernels  45.2 us (93%)
  local copies, waits for them, and re-layouts  2.42 us (5%)
  between operations  0.65 us (1%)
    pallas_call x1, Pallas kernels, local(): pl.pallas_call(kernel, out_shape=(jax.ShapeDtypeStruct(wide, BF16), jax.S...  45.2 us
    unnamed x4, local copies, waits for them, and re-layouts  2.42 us

profile of v2, /device:TPU:25, one launch (start us, length us, event | category | flops | bytes accessed | tf_op | source)
XLA Modules:
  0.0 48.2 jit_solution(18198692894741128664)
XLA Ops:
  0.6 45.2 %shard_map.104 = (bf16[512,256]{1,0:T(8,128)(2,1)}, bf16[512,256]{1,0:T(8,128)(2,1)}) custom-call(s32[4]{0:T(128)} %doc.1, bf16[512,256]{1,0:T(8,128)(2,1)} %lq_in.1, bf16[512,256]{1,0:T(8,128)(2,1)} %lk_in.1, bf16[512,256]{1,0:T(8,128)(2,1)} %lv_in.1, f32[2,512]{1,0:T(2,128)} %ld_in.1, f32[1,256]{1,0:T(1,128)} %bitcast.5, bf16[512,256]{1,0:T(8,128)(2,1)} %sq_in.1, ...), custom_call_target="tpu_custom_call" | custom-call | tf_op jit(solution)/shard_map/pallas_call | solution.py:336
  45.8 0.0 copy-start
  45.8 1.7 %copy.13 = bf16[512,256]{1,0:T(8,128)(2,1)} copy(bf16[512,256]{1,0:T(8,128)(2,1)} %get-tuple-element.4) | data formatting | bytes 524288
  47.5 0.0 copy-done
  47.5 0.7 %copy.14 = bf16[512,256]{1,0:T(8,128)(2,1)} copy(bf16[512,256]{1,0:T(8,128)(2,1)S(1)} %copy-done) | data formatting | bytes 524288
Async XLA Ops:
  45.8 1.7 %copy-start = (bf16[512,256]{1,0:T(8,128)(2,1)S(1)}, bf16[512,256]{1,0:T(8,128)(2,1)}, u32[]{:S(2)}) copy-start(bf16[512,256]{1,0:T(8,128)(2,1)} %get-tuple-element.5) | copy-start | bytes 786436

commit v3 on v2

--- a/solution.py
+++ b/solution.py
@@ -10,6 +10,7 @@
 DH = 128
 BLK = 256
 TOK = 512
+ROW_AT, COLUMN_AT = 4, 9
 NEAR = 9
 LOOK = 4
 REACH = 12
@@ -228,14 +229,18 @@
 
     def visit(d):
         keys, values = keys_of(d), values_of(d)
-        for t in range(4):
-            r = slice(t * HALF, (t + 1) * HALF)
-            s = mm(qx[r], keys)
-            old = top[r, :1]
+        tiles = [slice(t * HALF, (t + 1) * HALF) for t in range(2 * TOK // HALF)]
+        scores = mm(qx[tiles[0]], keys)
+        for t, r in enumerate(tiles):
+            s = scores
+            if t + 1 < len(tiles):
+                scores = mm(qx[tiles[t + 1]], keys)
+            old = top[r]
             m = jnp.maximum(old, jnp.max(s, axis=1, keepdims=True))
-            p = jnp.exp2((s - m) * SCALE).astype(BF16)
-            acc[r] = jnp.exp2((old - m) * SCALE) * acc[r] + mm(p, values, ABT)
-            top[r] = jnp.broadcast_to(m, (HALF, DH))
+            top[r] = m
+            p = jnp.exp2((s - jnp.concatenate([m] * (TOK // DH), axis=1)) * SCALE).astype(BF16)
+            shrink = jnp.exp2((old - m) * SCALE)
+            acc[r] = jnp.concatenate([shrink, shrink], axis=1) * acc[r] + mm(p, values, ABT)
 
     pass_own(2)
     arrived(0)
@@ -243,6 +248,17 @@
     for d in range(3, LOOK + 1):
         pass_own(d)
     pass_far(1)
+
+    def loop_body(d, c):
+        pass_own(d + LOOK)
+        pass_far(d + 1)
+        arrived(d)
+        visit(d)
+        return c
+
+    early = jnp.minimum(n_lo, ROW_AT)
+    late = jnp.minimum(n_lo, COLUMN_AT)
+    lax.fori_loop(1, early + 1, loop_body, 0)
 
     for k in range(1, 4):
         r_copy(k).wait_recv()
@@ -273,15 +289,7 @@
     n_down = 3 - line
     lax.fori_loop(1, n_down + 1, lambda k, c: (c_copy(k).start(), c)[1], 0)
 
-    def loop_body(d, c):
-        pass_own(d + LOOK)
-        pass_far(d + 1)
-        arrived(d)
-        visit(d)
-        return c
-
-    early = jnp.minimum(n_lo, 2)
-    lax.fori_loop(1, early + 1, loop_body, 0)
+    lax.fori_loop(early + 1, late + 1, loop_body, 0)
 
     def column(i, state):
         k = line - i
@@ -306,7 +314,7 @@
             if b == 0:
                 state = kept(base, base + BLK - 1) * through(0, h) * state + first_up[h]
 
-    lax.fori_loop(early + 1, n_lo + 1, loop_body, 0)
+    lax.fori_loop(late + 1, n_lo + 1, loop_body, 0)
 
     for t in range(4):
         r = slice(t * HALF, (t + 1) * HALF)

time: 48.7 us -> 38.1 us (0.78)
  Pallas kernels: 45.2 us -> 34.8 us
    pallas_call x1, Pallas kernels: 45.2 us -> 34.8 us  [local(): pl.pallas_call(kernel, out_shape=(jax.ShapeDtypeStruct(wide, BF16), jax.S...]
where the time goes in v3:
time: 38.1 us; the launch traced here: 37.9 us
  Pallas kernels  34.8 us (91%)
  local copies, waits for them, and re-layouts  2.42 us (6%)
  between operations  0.65 us (2%)
    pallas_call x1, Pallas kernels, local(): pl.pallas_call(kernel, out_shape=(jax.ShapeDtypeStruct(wide, BF16), jax.S...  34.8 us
    unnamed x4, local copies, waits for them, and re-layouts  2.42 us

profile of v3, /device:TPU:25, one launch (start us, length us, event | category | flops | bytes accessed | tf_op | source)
XLA Modules:
  0.0 37.9 jit_solution(8000288724100692476)
XLA Ops:
  0.6 34.8 %shard_map.104 = (bf16[512,256]{1,0:T(8,128)(2,1)}, bf16[512,256]{1,0:T(8,128)(2,1)}) custom-call(s32[4]{0:T(128)} %doc.1, bf16[512,256]{1,0:T(8,128)(2,1)} %lq_in.1, bf16[512,256]{1,0:T(8,128)(2,1)} %lk_in.1, bf16[512,256]{1,0:T(8,128)(2,1)} %lv_in.1, f32[2,512]{1,0:T(2,128)} %ld_in.1, f32[1,256]{1,0:T(1,128)} %bitcast.5, bf16[512,256]{1,0:T(8,128)(2,1)} %sq_in.1, ...), custom_call_target="tpu_custom_call" | custom-call | tf_op jit(solution)/shard_map/pallas_call | solution.py:344
  35.4 0.0 copy-start
  35.5 1.7 %copy.13 = bf16[512,256]{1,0:T(8,128)(2,1)} copy(bf16[512,256]{1,0:T(8,128)(2,1)} %get-tuple-element.4) | data formatting | bytes 524288
  37.2 0.0 copy-done
  37.2 0.7 %copy.14 = bf16[512,256]{1,0:T(8,128)(2,1)} copy(bf16[512,256]{1,0:T(8,128)(2,1)S(1)} %copy-done) | data formatting | bytes 524288
Async XLA Ops:
  35.4 1.7 %copy-start = (bf16[512,256]{1,0:T(8,128)(2,1)S(1)}, bf16[512,256]{1,0:T(8,128)(2,1)}, u32[]{:S(2)}) copy-start(bf16[512,256]{1,0:T(8,128)(2,1)} %get-tuple-element.5) | copy-start | bytes 786436

commit v4 on v3

--- a/solution.py
+++ b/solution.py
@@ -11,7 +11,7 @@
 BLK = 256
 TOK = 512
 ROW_AT, COLUMN_AT = 4, 9
-NEAR = 9
+PAIRED = 3
 LOOK = 4
 REACH = 12
 HALF = 256
@@ -34,7 +34,7 @@
     lin_out, soft_out,
     lq, lk, lv, ld, gain, sq,
     kv, qx, top, acc, raw, cum, row_st, col_st, first_up, carry,
-    in_sem, x_send, x_recv, y_send, s_send, s_recv, z_send, z_recv, t_send, t_recv,
+    in_sem, x_send, x_recv, y_send, a_send, s_send, s_recv, z_send, z_recv, t_send, t_recv,
     r_send, r_recv, c_send, c_recv,
 ):
     me = lax.axis_index("ctx")
@@ -64,11 +64,12 @@
     greet(me, sib)
     greet(me, zp)
     lax.fori_loop(1, n_lo + 1, lambda d, c: (greet(me - d, hd), c)[1], 0)
-    lax.fori_loop(1, n_hi + 1, lambda d, c: (greet(me + d, hd), c)[1], 0)
+    right = jnp.where(line < 3, 3 - col, 0)
+    lax.fori_loop(1, right + 1, lambda k, c: (greet(me + k, hd), c)[1], 0)
 
     loads[0].wait()
     loads[1].wait()
-    pl.semaphore_wait(barrier, 2 + n_lo + n_hi)
+    pl.semaphore_wait(barrier, 2 + n_hi + jnp.where(line < 3, col, 0))
 
     def copy(src, dst, send, recv, ctx, head):
         return pltpu.make_async_remote_copy(
@@ -76,10 +77,44 @@
         )
 
     def x_copy(d):
-        return copy(kv.at[0, quarter], kv.at[d, quarter], x_send.at[d], x_recv.at[d], me + d, hd)
-
-    def y_copy(d):
-        return copy(kv.at[0, zquarter], kv.at[d, zquarter], y_send.at[d], z_recv.at[d], me + d, hd)
+        return copy(kv.at[0, quarter], kv.at[d, quarter], x_send.at[0], x_recv.at[d], me, sib)
+
+    def down(k):
+        return copy(kv.at[0, quarter], kv.at[4 * k, quarter], x_send.at[k], x_recv.at[4 * k], me + 4 * k, hd)
+
+    def down_far():
+        d = 4 * PAIRED
+        return copy(kv.at[0, zquarter], kv.at[d, zquarter], y_send.at[0], z_recv.at[d], me + d, hd)
+
+    def aside(k, shift):
+        d = 4 * k + shift
+        return copy(kv.at[4 * k, quarter], kv.at[d, quarter], a_send.at[k, shift + 3], x_recv.at[d], me + shift, hd)
+
+    def near(shift):
+        d = 4 + shift
+        return copy(kv.at[0, quarter], kv.at[d, quarter], a_send.at[1, shift + 3], x_recv.at[d], me + d, hd)
+
+    def all_near(use):
+        for shift in range(-3, 4):
+
+            @pl.when((line < 3) & (col + shift >= 0) & (col + shift <= 3))
+            def _():
+                use(shift)
+
+    def aside_far(shift):
+        k, d = PAIRED, 4 * PAIRED + shift
+        return copy(kv.at[4 * k, zquarter], kv.at[d, zquarter], y_send.at[shift + 4], z_recv.at[d], me + shift, hd)
+
+    def far(d):
+        return line - (me - d) // 4 == PAIRED
+
+    def all_aside(k, use):
+        for shift in range(-3, 4):
+            if shift and 1 <= 4 * k + shift <= REACH:
+
+                @pl.when((line >= k) & (col + shift >= 0) & (col + shift <= 3))
+                def _():
+                    use(shift)
 
     def s_copy(d):
         return copy(kv.at[d, quarter], kv.at[d, quarter], s_send.at[d], s_recv.at[d], me, sib)
@@ -99,9 +134,9 @@
     def pass_own(d):
         @pl.when(d <= n_lo)
         def _():
-            x_copy(d).wait_recv()
+            pl.when((d != 8) & (d != 12))(lambda: x_copy(d).wait_recv())
             s_copy(d).start()
-            pl.when(d <= NEAR)(lambda: z_copy(d).start())
+            pl.when(~far(d))(lambda: z_copy(d).start())
 
     def pass_far(d):
         @pl.when(d <= n_lo)
@@ -111,7 +146,14 @@
 
     s_copy(0).start()
     z_copy(0).start()
-    lax.fori_loop(1, n_hi + 1, lambda d, c: (x_copy(d).start(), c)[1], 0)
+    n_down = 3 - line
+    all_aside(0, lambda shift: aside(0, shift).start())
+    lax.fori_loop(2, n_down + 1, lambda k, c: (down(k).start(), c)[1], 0)
+    all_near(lambda shift: near(shift).start())
+
+    def spread(k):
+        pl.when(line >= k)(lambda: x_copy(4 * k).wait_recv())
+        all_aside(k, lambda shift: aside(k, shift).start())
 
     bounds = [doc[0], doc[0] + doc[1], doc[0] + doc[1] + doc[2]]
 
@@ -181,7 +223,9 @@
         row_st[0, h * DH : (h + 1) * DH] = whole.astype(BF16)
         if h == 0:
             pass_far(0)
-            lax.fori_loop(NEAR + 1, n_hi + 1, lambda d, c: (y_copy(d).start(), c)[1], 0)
+            pl.when(line + PAIRED <= 3)(lambda: down_far().start())
+            for k in range(2, 4):
+                spread(k)
             pass_own(1)
     pad_row = lax.broadcasted_iota(jnp.int32, (16, DH), 0)
 
@@ -194,7 +238,7 @@
 
     row_st[0, 2 * DH :] = factor_rows(through(0, 0) * through(1, 0), through(0, 1) * through(1, 1))
     for k in range(1, 4):
-        r_copy(k).start()
+        pl.when((line < 3) | (col + k <= 3))(lambda: r_copy(k).start())
 
     def factor_of(block, h):
         tail = block[2 * DH :].astype(F32)
@@ -242,6 +286,8 @@
             shrink = jnp.exp2((old - m) * SCALE)
             acc[r] = jnp.concatenate([shrink, shrink], axis=1) * acc[r] + mm(p, values, ABT)
 
+    pass_far(4 * PAIRED)
+    all_aside(PAIRED, lambda shift: aside_far(shift).start())
     pass_own(2)
     arrived(0)
     diagonal()
@@ -251,7 +297,7 @@
 
     def loop_body(d, c):
         pass_own(d + LOOK)
-        pass_far(d + 1)
+        pl.when(d + 1 != 4 * PAIRED)(lambda: pass_far(d + 1))
         arrived(d)
         visit(d)
         return c
@@ -261,7 +307,7 @@
     lax.fori_loop(1, early + 1, loop_body, 0)
 
     for k in range(1, 4):
-        r_copy(k).wait_recv()
+        pl.when((line < 3) | (col >= k))(lambda: r_copy(k).wait_recv())
     line_first = line * 4 * TOK
     enter_row = []
     enter_factor = []
@@ -286,7 +332,6 @@
         enter_row.append(plain)
         col_st[0, h * DH : (h + 1) * DH] = total.astype(BF16)
     col_st[0, 2 * DH :] = factor_rows(enter_row[0], enter_row[1])
-    n_down = 3 - line
     lax.fori_loop(1, n_down + 1, lambda k, c: (c_copy(k).start(), c)[1], 0)
 
     lax.fori_loop(early + 1, late + 1, loop_body, 0)
@@ -324,15 +369,19 @@
 
     def sent(d, c):
         s_copy(d).wait_send()
-        pl.when(d <= NEAR)(lambda: z_copy(d).wait_send())
+        pl.when(~far(d))(lambda: z_copy(d).wait_send())
         t_copy(d).wait_send()
         return c
 
     lax.fori_loop(0, n_lo + 1, sent, 0)
-    lax.fori_loop(1, n_hi + 1, lambda d, c: (x_copy(d).wait_send(), c)[1], 0)
-    lax.fori_loop(NEAR + 1, n_hi + 1, lambda d, c: (y_copy(d).wait_send(), c)[1], 0)
+    lax.fori_loop(2, n_down + 1, lambda k, c: (down(k).wait_send(), c)[1], 0)
+    all_near(lambda shift: near(shift).wait_send())
+    pl.when(line + PAIRED <= 3)(lambda: down_far().wait_send())
+    for k in (0, 2, 3):
+        all_aside(k, lambda shift: aside(k, shift).wait_send())
+    all_aside(PAIRED, lambda shift: aside_far(shift).wait_send())
     for k in range(1, 4):
-        r_copy(k).wait_send()
+        pl.when((line < 3) | (col + k <= 3))(lambda: r_copy(k).wait_send())
     lax.fori_loop(1, n_down + 1, lambda k, c: (c_copy(k).wait_send(), c)[1], 0)
 
 
@@ -353,7 +402,7 @@
             vmem((2 * TOK, 2 * DH), F32), vmem(wide, F32), vmem((BLK, 8), F32),
             vmem((4, 2 * DH + 16, DH), BF16), vmem((4, 2 * DH + 16, DH), BF16), vmem((2, DH, DH), F32),
             vmem((2, DH, DH), F32),
-            dma((8,)), dma((slots,)), dma((slots,)), dma((slots,)), dma((slots,)), dma((slots,)), dma((slots,)),
+            dma((8,)), dma((4,)), dma((slots,)), dma((8,)), dma((4, 7)), dma((slots,)), dma((slots,)), dma((slots,)),
             dma((slots,)), dma((slots,)), dma((slots,)), dma((4,)), dma((4,)), dma((4,)), dma((4,)),
         ],
         compiler_params=pltpu.CompilerParams(

time: 38.1 us -> 37.8 us (level)
  no operation moved by 1% of the time
where the time goes in v4:
time: 37.8 us; the launch traced here: 37.6 us
  Pallas kernels  34.5 us (91%)
  local copies, waits for them, and re-layouts  2.42 us (6%)
  between operations  0.65 us (2%)
    pallas_call x1, Pallas kernels, local(): pl.pallas_call(kernel, out_shape=(jax.ShapeDtypeStruct(wide, BF16), jax.S...  34.5 us
    unnamed x4, local copies, waits for them, and re-layouts  2.42 us

profile of v4, /device:TPU:25, one launch (start us, length us, event | category | flops | bytes accessed | tf_op | source)
XLA Modules:
  0.0 37.6 jit_solution(14142454547101771761)
XLA Ops:
  0.6 34.5 %shard_map.104 = (bf16[512,256]{1,0:T(8,128)(2,1)}, bf16[512,256]{1,0:T(8,128)(2,1)}) custom-call(s32[4]{0:T(128)} %doc.1, bf16[512,256]{1,0:T(8,128)(2,1)} %lq_in.1, bf16[512,256]{1,0:T(8,128)(2,1)} %lk_in.1, bf16[512,256]{1,0:T(8,128)(2,1)} %lv_in.1, f32[2,512]{1,0:T(2,128)} %ld_in.1, f32[1,256]{1,0:T(1,128)} %bitcast.5, bf16[512,256]{1,0:T(8,128)(2,1)} %sq_in.1, ...), custom_call_target="tpu_custom_call" | custom-call | tf_op jit(solution)/shard_map/pallas_call | solution.py:393
  35.2 0.0 copy-start
  35.2 1.7 %copy.13 = bf16[512,256]{1,0:T(8,128)(2,1)} copy(bf16[512,256]{1,0:T(8,128)(2,1)} %get-tuple-element.4) | data formatting | bytes 524288
  36.9 0.0 copy-done
  36.9 0.7 %copy.14 = bf16[512,256]{1,0:T(8,128)(2,1)} copy(bf16[512,256]{1,0:T(8,128)(2,1)S(1)} %copy-done) | data formatting | bytes 524288
Async XLA Ops:
  35.2 1.7 %copy-start = (bf16[512,256]{1,0:T(8,128)(2,1)S(1)}, bf16[512,256]{1,0:T(8,128)(2,1)}, u32[]{:S(2)}) copy-start(bf16[512,256]{1,0:T(8,128)(2,1)} %get-tuple-element.5) | copy-start | bytes 786436

commit v5 on v4

--- a/solution.py
+++ b/solution.py
@@ -12,7 +12,7 @@
 TOK = 512
 ROW_AT, COLUMN_AT = 4, 9
 PAIRED = 3
-LOOK = 4
+LOOK = 3
 REACH = 12
 HALF = 256
 BIG = 1048576.0

time: 37.8 us -> 39.3 us (1.040); the launches traced: 37.6 us -> 38.7 us
  Pallas kernels: 34.5 us -> 35.6 us
    pallas_call x1, Pallas kernels: 34.5 us -> 35.6 us  [local(): pl.pallas_call(kernel, out_shape=(jax.ShapeDtypeStruct(wide, BF16), jax.S...]
where the time goes in v5:
time: 39.3 us; the launch traced here: 38.7 us
  Pallas kernels  35.6 us (91%)
  local copies, waits for them, and re-layouts  2.42 us (6%)
  between operations  0.65 us (2%)
    pallas_call x1, Pallas kernels, local(): pl.pallas_call(kernel, out_shape=(jax.ShapeDtypeStruct(wide, BF16), jax.S...  35.6 us
    unnamed x4, local copies, waits for them, and re-layouts  2.42 us

profile of v5, /device:TPU:25, one launch (start us, length us, event | category | flops | bytes accessed | tf_op | source)
XLA Modules:
  0.0 38.7 jit_solution(14925658503951857741)
XLA Ops:
  0.6 35.6 %shard_map.104 = (bf16[512,256]{1,0:T(8,128)(2,1)}, bf16[512,256]{1,0:T(8,128)(2,1)}) custom-call(s32[4]{0:T(128)} %doc.1, bf16[512,256]{1,0:T(8,128)(2,1)} %lq_in.1, bf16[512,256]{1,0:T(8,128)(2,1)} %lk_in.1, bf16[512,256]{1,0:T(8,128)(2,1)} %lv_in.1, f32[2,512]{1,0:T(2,128)} %ld_in.1, f32[1,256]{1,0:T(1,128)} %bitcast.5, bf16[512,256]{1,0:T(8,128)(2,1)} %sq_in.1, ...), custom_call_target="tpu_custom_call" | custom-call | tf_op jit(solution)/shard_map/pallas_call | solution.py:393
  36.3 0.0 copy-start
  36.3 1.7 %copy.13 = bf16[512,256]{1,0:T(8,128)(2,1)} copy(bf16[512,256]{1,0:T(8,128)(2,1)} %get-tuple-element.4) | data formatting | bytes 524288
  38.0 0.0 copy-done
  38.0 0.7 %copy.14 = bf16[512,256]{1,0:T(8,128)(2,1)} copy(bf16[512,256]{1,0:T(8,128)(2,1)S(1)} %copy-done) | data formatting | bytes 524288
Async XLA Ops:
  36.3 1.7 %copy-start = (bf16[512,256]{1,0:T(8,128)(2,1)S(1)}, bf16[512,256]{1,0:T(8,128)(2,1)}, u32[]{:S(2)}) copy-start(bf16[512,256]{1,0:T(8,128)(2,1)} %get-tuple-element.5) | copy-start | bytes 786436
